TPU v7x, 32 devices: a whole 2x2x4 slice. The times are simulated.
32 devices in a mesh: tens: 2 (over y), atom: 16 (over z, x, core).
Axes of the slice: x: 2, y: 2, z: 4, core: 2. Of those that a mesh axis runs over, the one named last changes fastest.
Arguments:
- chibar: float32 [96, 4096], P(None, 'atom'), may hold values from -6 to 6
- t_blocks: float32 [384, 196608], P(None, ('tens', 'atom')), may hold values from -0.3125 to 0.3125
- n_saved: float32 [96, 196608], P('tens', 'atom'), may hold values from -0.078125 to 0.078125
- q_list: int32 [2, 16, 3], P('tens', 'atom'), may hold values from 0 to 13, as said below
- q_count: int32 [2, 16], P('tens', 'atom'), may hold values from 1 to 3, as said below
Outputs:
- gbar: float32 [1024, 320], P('atom')
Inputs may be any that keep to these rules, and one draw needn't show every extreme that they name: `q_list`: the 3 entries of one pair owner's list name blocks of 3 distinct atom indices. `q_count`: equal to 3 on at least one pair owner.
All inputs are finite; a program needn't handle non-finite values.
Results may differ from a plain program's by a relative error of at most 0.0003.
Values sent between devices are 32-bit elements; how exact they have to be, the bound alone decides.
No kernel may reach another device: no remote copies, remote signals or barrier semaphores. Data moves between devices by JAX's collectives and lax.ppermute only.
A program may use at most 64 MiB of HBM per device.

v0:
```python
import jax
import jax.numpy as jnp
from jax import lax
from jax.experimental import pallas as pl
from jax.experimental.pallas import tpu as pltpu
from jax.sharding import PartitionSpec as P


LANES = 128
SUBL = 8
REACH = 3
VM = pl.BlockSpec(memory_space=pltpu.VMEM)
SM = pl.BlockSpec(memory_space=pltpu.SMEM)
HB = pl.BlockSpec(memory_space=pltpu.HBM)
f32 = jnp.float32
bf16 = jnp.bfloat16


def limit(mib):
    return pltpu.CompilerParams(vmem_limit_bytes=mib * 2**20)


def vmem(shape, dtype):
    return pltpu.VMEM(shape, dtype)


def split(x):
    hi = x.astype(bf16)
    return hi, (x - hi.astype(f32)).astype(bf16)


def shift(x, by):
    atoms = lax.axis_size("atom")
    return lax.ppermute(x, "atom", [(i, (i + by) % atoms) for i in range(atoms)])


def send(x, to):
    atoms = lax.axis_size("atom")
    pairs = []
    for t in range(2):
        for s in range(atoms):
            u, v = to(t, s)
            pairs.append((t * atoms + s, u * atoms + v % atoms))
    return lax.ppermute(x, ("tens", "atom"), pairs)


def prep_t(t_blocks):
    rows, cols = t_blocks.shape
    step = 64

    def body(src, hi, lo, buf, sems):
        copies = []
        for i in range(rows // step):
            here = pl.ds(i * step, step)
            copies.append(pltpu.make_async_copy(src.at[here], buf.at[here], sems.at[i]))
            copies[-1].start()
        for i in range(rows // step):
            copies[i].wait()

            def tile(c, carry, i=i):
                at = pl.ds(pl.multiple_of(c * 512, 512), 512)
                here = pl.ds(i * step, step)
                h, l = split(buf[here, at])
                hi[here, at] = h
                lo[here, at] = l
                return carry

            lax.fori_loop(0, cols // 512, tile, 0)

    return pl.pallas_call(
        body, in_specs=[HB], out_specs=[VM, VM],
        out_shape=[vmem((rows, cols), bf16), vmem((rows, cols), bf16)],
        scratch_shapes=[pltpu.VMEM((rows, cols), f32), pltpu.SemaphoreType.DMA((rows // step,))],
        name="prep_t", compiler_params=limit(14),
    )(t_blocks)


def head(x, rows):
    def body(src, out, sem):
        copy = pltpu.make_async_copy(src.at[pl.ds(0, rows)], out, sem)
        copy.start()
        copy.wait()

    return pl.pallas_call(
        body, in_specs=[HB], out_specs=VM, out_shape=vmem((rows, x.shape[1]), x.dtype),
        scratch_shapes=[pltpu.SemaphoreType.DMA], name="head", compiler_params=limit(4),
    )(x)


def prep_n(saved, orb):
    rows, cols = saved.shape
    groups = rows // SUBL
    half = LANES // 2
    pairs = orb // 2
    wide = 2 * LANES

    def body(src, hi, lo, buf, tiles, tmp, sems):
        def copy(i):
            here = pl.ds(pl.multiple_of(i * SUBL, SUBL), SUBL)
            return pltpu.make_async_copy(src.at[here], buf.at[here], sems.at[i])

        for i in range(groups):
            copy(i).start()
        low = lax.broadcasted_iota(jnp.int32, (pairs, LANES), 1) < half

        def group(i, carry):
            copy(i).wait()
            here = pl.ds(pl.multiple_of(i * SUBL, SUBL), SUBL)
            for c in range(cols // LANES):
                tiles[c * SUBL:(c + 1) * SUBL, :] = buf[here, c * LANES:(c + 1) * LANES]
            for r in range(SUBL):
                v = [tiles[pl.ds(k * SUBL + r, pairs, stride=3 * SUBL), :] for k in range(3)]
                w1, w2 = (pltpu.roll(x, half, 1) for x in v[1:])
                tmp[r, 0, pl.ds(0, pairs, stride=2), :] = v[0]
                tmp[r, 1, pl.ds(0, pairs, stride=2), :] = v[1]
                tmp[r, 0, pl.ds(1, pairs, stride=2), :] = jnp.where(low, w1, w2)
                tmp[r, 1, pl.ds(1, pairs, stride=2), :] = w2
                at = pl.ds(pl.multiple_of(i * SUBL * orb + r * orb, orb), orb)
                for k in range(2):
                    h, l = split(tmp[r, k])
                    hi[at, k * LANES:(k + 1) * LANES] = h
                    lo[at, k * LANES:(k + 1) * LANES] = l
            return carry

        lax.fori_loop(0, groups, group, 0)

    return pl.pallas_call(
        body, in_specs=[HB], out_specs=[VM, VM],
        out_shape=[vmem((rows * orb, wide), bf16)] * 2,
        scratch_shapes=[pltpu.VMEM((rows, cols), f32), pltpu.VMEM((cols // LANES * SUBL, LANES), f32),
                        pltpu.VMEM((SUBL, 2, orb, LANES), f32), pltpu.SemaphoreType.DMA((groups,))],
        name="prep_n", compiler_params=limit(10),
    )(saved)


def select(pieces, q_list, q_count, p_rows, early, after):
    p_all, width = pieces[0].shape
    ql = q_list.shape[-1]
    blk = LANES
    qb = width // blk

    def body(*refs):
        parts, (ql_ref, qc_ref, _, out, scr) = refs[:len(pieces)], refs[len(pieces):]
        t = lax.axis_index("tens")
        for q in range(ql):
            want = ql_ref[0, 0, q]
            pick = parts[0][:, :blk]
            for i in range(1, len(parts) * qb):
                pick = jnp.where(want == i, parts[i // qb][:, (i % qb) * blk:(i % qb + 1) * blk], pick)
            scr[:, q * blk:(q + 1) * blk] = jnp.where(q < qc_ref[0, 0], pick, 0.0)
        other = (1 - t) * p_rows
        order = ((other + early, p_rows - early), (t * p_rows, p_rows), (other, early))
        at = 0
        for start, size in order:
            h, l = split(scr[pl.ds(pl.multiple_of(start, 16), size), :])
            out[at:at + size, :] = h
            out[p_all + at:p_all + at + size, :] = l
            at += size

    return pl.pallas_call(
        body, in_specs=[VM] * len(pieces) + [SM, SM, VM], out_specs=VM,
        out_shape=vmem((2 * p_all, ql * blk), bf16),
        scratch_shapes=[pltpu.VMEM((p_all, ql * blk), f32)], name="select", compiler_params=limit(8),
    )(*pieces, q_list, q_count, after)


def multiply(chosen, t_hi, t_lo, first, slope, cols, cross):
    p_all = chosen.shape[0] // 2
    own = p_all - cross
    ct = cols // LANES
    sub = 512 if cols % 512 == 0 else 256

    def body(c, hi, lo, out_c, out_o):
        start = first + slope * lax.axis_index("tens")
        for j in range(cols // sub):
            at = pl.ds(pl.multiple_of(start + j * sub, LANES), sub)
            big = jnp.dot(c[...], hi[:, at], preferred_element_type=f32)
            val = big[:p_all] + big[p_all:] + jnp.dot(c[:p_all, :], lo[:, at], preferred_element_type=f32)
            for k in range(sub // LANES):
                jt = j * (sub // LANES) + k
                for i in range(p_all // SUBL):
                    v = val[i * SUBL:(i + 1) * SUBL, k * LANES:(k + 1) * LANES]
                    if i < cross // SUBL:
                        out_c[pl.ds((i * ct + jt) * SUBL, SUBL), :] = v
                    else:
                        out_o[pl.ds(((i - cross // SUBL) * ct + jt) * SUBL, SUBL), :] = v

    return pl.pallas_call(
        body, in_specs=[VM] * 3, out_specs=[VM, VM],
        out_shape=[vmem((cross * ct, LANES), f32), vmem((own * ct, LANES), f32)], name="multiply", compiler_params=limit(8),
    )(chosen, t_hi, t_lo)


def contract_into(x, rows, ct, n_parts, n_rows, l_hi, l_lo):
    lane = lax.broadcasted_iota(jnp.int32, (ct, LANES), 1)
    low = lane < LANES // 2
    for p in range(0, rows, 2):
        a, b = (x[pl.ds((q // SUBL) * ct * SUBL + q % SUBL, ct, stride=SUBL), :] for q in (p, p + 1))
        even = jnp.where(low, a, pltpu.roll(b, LANES // 2, 1))
        odd = jnp.where(low, pltpu.roll(a, LANES // 2, 1), b)
        at = pl.ds((p // 2) * LANES, LANES)
        for i, v in enumerate((even, odd)):
            h, l = split(v)
            l_hi[pl.ds(i * ct, ct), at] = h
            l_lo[pl.ds(i * ct, ct), at] = l
    half = LANES // 2
    total = None
    at = 0
    for (w_hi, w_lo), (start, count) in zip(n_parts, n_rows):
        k = pl.ds(at * half, count * half)
        w = pl.ds(start * half, count * half)
        v = jnp.dot(l_hi[:, k], w_hi[w, :], preferred_element_type=f32)
        v += jnp.dot(l_lo[:, k], w_hi[w, :], preferred_element_type=f32)
        v += jnp.dot(l_hi[:, k], w_lo[w, :], preferred_element_type=f32)
        total = v if total is None else total + v
        at += count
    return total


def contract(stretches, rows, saved, n_rows, band, sizes, after=()):
    wide = -(-band // LANES)
    cts = [x.shape[0] // rows for x in stretches]
    flat = [w for pair in saved for w in pair]

    def body(*refs):
        refs = list(refs)
        xs = [refs.pop(0) for _ in stretches]
        ws = [refs.pop(0) for _ in flat]
        del refs[:len(after)]
        outs = [refs.pop(0) for _ in sizes]
        acc = refs.pop(0)
        pairs = list(zip(ws[0::2], ws[1::2]))
        base = 0
        for i, (x, ct) in enumerate(zip(xs, cts)):
            val = contract_into(x, rows, ct, pairs, n_rows, refs[2 * i], refs[2 * i + 1])
            for par in range(2):
                for c in range(wide):
                    acc[c, pl.ds(base + par, ct, stride=2), :] = val[par * ct:(par + 1) * ct, c * LANES:(c + 1) * LANES]
            base += 2 * ct
        at = 0
        for out, size in zip(outs, sizes):
            out[...] = jnp.concatenate([acc[c, at:at + size, :] for c in range(wide)], axis=1)[:, :band]
            at += size

    scratch = [pltpu.VMEM((wide, 2 * sum(cts), LANES), f32)]
    for x, ct in zip(stretches, cts):
        scratch += [pltpu.VMEM((2 * ct, rows * LANES // 2), bf16)] * 2
    return pl.pallas_call(
        body, in_specs=[VM] * (len(stretches) + len(flat) + len(after)), out_specs=[VM] * len(sizes),
        out_shape=[vmem((size, band), f32) for size in sizes], scratch_shapes=scratch,
        name="contract", compiler_params=limit(12),
    )(*stretches, *flat, *after)


def finish(own, rec, orb, band):
    def body(ho, oa, ob, oc, hr, ra, rb, rc, out):
        t = lax.axis_index("tens")
        first = t == 0
        lower = jnp.where(first, ob[...], oa[...]) + jnp.where(first, ra[...], rb[...])
        upper = jnp.where(first, oa[...], ob[...]) + jnp.where(first, rb[...], ra[...])
        x = ho[...] + rc[...]
        y = oc[...] + hr[...]
        mid = jnp.concatenate([jnp.where(first, x, y), jnp.where(first, y, x)], axis=0)
        zero = jnp.zeros((orb, orb), f32)
        out[...] = (jnp.concatenate([lower, zero, zero], axis=1) + jnp.concatenate([zero, mid, zero], axis=1)
                    + jnp.concatenate([zero, zero, upper], axis=1))

    return pl.pallas_call(
        body, in_specs=[VM] * 8, out_specs=VM,
        out_shape=jax.ShapeDtypeStruct((orb, band + 2 * orb), f32), name="finish", compiler_params=limit(8),
    )(*own, *rec)


def paired(chibar, t_blocks, n_saved, q_list, q_count):
    p_rows, n_cols = n_saved.shape
    orb = LANES // 2
    band = n_cols // orb
    nu_t = t_blocks.shape[1] // orb
    early = 16
    cross = p_rows - early
    swap = [(0, 1), (1, 0)]

    n_saved = pltpu.with_memory_space_constraint(n_saved, pltpu.HBM)
    t_blocks = pltpu.with_memory_space_constraint(t_blocks, pltpu.HBM)
    n_far = lax.ppermute(head(n_saved, early), "tens", swap)
    pieces = [chibar if o == 0 else shift(chibar, -o) for o in range(-REACH, REACH + 1)]
    t_hi, t_lo = prep_t(t_blocks)
    near = prep_n(n_saved, orb)
    chosen = select(pieces, q_list, q_count, p_rows, early, near[0])

    rest = nu_t - orb
    far_main, own_main = multiply(chosen, t_hi, t_lo, 0, rest * orb, orb * orb, cross)
    far_main = lax.ppermute(far_main, "tens", swap)
    far_rest, own_rest = multiply(chosen, t_hi, t_lo, orb * orb, -orb * orb, rest * orb, cross)
    far_rest = lax.ppermute(far_rest, "tens", swap)

    beyond = prep_n(n_far, orb)
    o_main, o_rest = contract([own_main, own_rest], p_rows + early, [near, beyond], [(0, p_rows), (0, early)],
                              band, [orb, rest])
    oa = send(o_main, lambda t, s: (t, s - 1 + 2 * t))
    ob = send(o_main, lambda t, s: (1 - t, s - 1 + 2 * t))
    oc = send(o_rest, lambda t, s: (1 - t, s))
    r_main, = contract([far_main], cross, [near], [(early, cross)], band, [orb], after=(o_rest,))
    ra = send(r_main, lambda t, s: (t, s + 1 - 2 * t))
    rb = send(r_main, lambda t, s: (1 - t, s + 1 - 2 * t))
    r_rest, = contract([far_rest], cross, [near], [(early, cross)], band, [rest])
    rc = send(r_rest, lambda t, s: (1 - t, s))
    return finish((o_rest, oa, ob, oc), (r_rest, ra, rb, rc), orb, band)


def general(chibar, t_blocks, n_saved, q_list, q_count):
    tens = lax.axis_size("tens")
    t = lax.axis_index("tens")
    p_rows, n_cols = n_saved.shape
    blk = t_blocks.shape[0] // q_list.shape[-1]
    ql = q_list.shape[-1]
    qb = chibar.shape[1] // blk
    reach = REACH
    orb = int(round((n_cols // 3) ** 0.5))
    band = 3 * orb
    nu_t = t_blocks.shape[1] // orb
    high = lax.Precision.HIGH
    slot_ids = q_list.reshape(ql)
    in_use = q_count.reshape(())
    keeper = jnp.arange(ql) < in_use

    def chosen_of(r):
        rows = lax.dynamic_slice_in_dim(chibar, ((t + r) % tens) * p_rows, p_rows, 0)
        pieces = [rows if o == 0 else shift(rows, -o) for o in range(-reach, reach + 1)]
        blocks = [pc[:, b * blk:(b + 1) * blk] for pc in pieces for b in range(qb)]
        out = []
        for q in range(ql):
            pick = blocks[0]
            for i in range(1, len(blocks)):
                pick = jnp.where(slot_ids[q] == i, blocks[i], pick)
            out.append(jnp.where(keeper[q], pick, 0.0))
        return jnp.concatenate(out, axis=1)

    saved = n_saved.reshape(p_rows, orb, band)
    parts = []
    mb = []
    for r in list(range(1, tens)) + [0]:
        m = jnp.dot(chosen_of(r), t_blocks, precision=high, preferred_element_type=jnp.float32)
        if r:
            m = lax.ppermute(m, "tens", [(i, (i + r) % tens) for i in range(tens)])
        mb.append(m)
    mb = [mb[-1]] + mb[:-1]
    for r in range(tens):
        parts.append(jnp.einsum("pnm,pml->nl", mb[r].reshape(p_rows, nu_t, orb), saved, precision=high,
                                preferred_element_type=jnp.float32))
    stacked = jnp.stack(parts)
    order = (t - jnp.arange(tens)) % tens
    if tens == 2:
        partial = jnp.where(t == 0, stacked, stacked[::-1]).reshape(band, band)
    else:
        partial = jnp.take(stacked, order, axis=0).reshape(band, band)
    blocks = partial.reshape(3, orb, band)
    lower = shift(blocks[2], 1)
    upper = shift(blocks[0], -1)
    pad = lambda x, o: jnp.pad(x, ((0, 0), (o * orb, (2 - o) * orb)))
    res = pad(lower, 0) + pad(blocks[1], 1) + pad(upper, 2)
    if tens == 2:
        return res + lax.ppermute(res, "tens", [(0, 1), (1, 0)])
    return lax.psum(res, "tens")


def solution(mesh):
    placed = (
        P(None, "atom"),
        P(None, ("tens", "atom")),
        P("tens", "atom"),
        P("tens", "atom", None),
        P("tens", "atom"),
    )

    def program(body):
        return jax.shard_map(body, mesh=mesh, in_specs=placed, out_specs=P("atom", None), check_vma=False)

    if mesh.shape["tens"] != 2:
        return program(general)

    return program(paired)
```

profile of v0, /device:TPU:0, one launch (start us, length us, event | category | flops | bytes accessed | tf_op | source)
XLA Modules:
  0.0 64.5 jit_solution(9784346407285427884)
XLA Ops:
  0.0 1.1 %head.1 = f32[16,12288]{1,0:T(8,128)S(1)} custom-call(f32[48,12288]{1,0:T(8,128)} %src.5), custom_call_target="tpu_custom_call" | custom-call | tf_op jit(solution)/shard_map/head/pallas_call | solution.py:84
  1.1 3.1 %collective-permute-start.6 = (f32[16,12288]{1,0:T(8,128)S(1)}, f32[16,12288]{1,0:T(8,128)S(1)}, u32[]{:S(2)}, u32[]{:S(2)}) collective-permute-start(f32[16,12288]{1,0:T(8,128)S(1)} %head.1), channel_id=1, source_target_pairs={{0,16},{16,0},{1,17},{17,1},{2,18},{18,2},{3,19},{19,3},{4,20},{20... | collective-permute-start | bytes 2359304 | tf_op jit(solution)/shard_map/ppermute | solution.py:285
  4.2 0.7 %collective-permute-start = (f32[96,256]{1,0:T(8,128)}, f32[96,256]{1,0:T(8,128)S(1)}, u32[]{:S(2)}, u32[]{:S(2)}) collective-permute-start(f32[96,256]{1,0:T(8,128)} %refs_3_.1), channel_id=1, source_target_pairs={{0,3},{1,4},{2,5},{3,6},{4,7},{5,8},{6,9},{7,10},{8,11},{9,12},{10... | collective-permute-start | bytes 294920 | tf_op jit(solution)/shard_map/ppermute | solution.py:34
  4.9 1.5 %collective-permute-start.1 = (f32[96,256]{1,0:T(8,128)}, f32[96,256]{1,0:T(8,128)S(1)}, u32[]{:S(2)}, u32[]{:S(2)}) collective-permute-start(f32[96,256]{1,0:T(8,128)} %refs_3_.1), channel_id=1, source_target_pairs={{0,2},{1,3},{2,4},{3,5},{4,6},{5,7},{6,8},{7,9},{8,10},{9,11},{10,... | collective-permute-start | bytes 294920 | tf_op jit(solution)/shard_map/ppermute | solution.py:34
  6.4 0.7 %collective-permute-start.2 = (f32[96,256]{1,0:T(8,128)}, f32[96,256]{1,0:T(8,128)S(1)}, u32[]{:S(2)}, u32[]{:S(2)}) collective-permute-start(f32[96,256]{1,0:T(8,128)} %refs_3_.1), channel_id=1, source_target_pairs={{0,1},{1,2},{2,3},{3,4},{4,5},{5,6},{6,7},{7,8},{8,9},{9,10},{10,1... | collective-permute-start | bytes 294920 | tf_op jit(solution)/shard_map/ppermute | solution.py:34
  7.1 3.7 %collective-permute-start.3 = (f32[96,256]{1,0:T(8,128)}, f32[96,256]{1,0:T(8,128)S(1)}, u32[]{:S(2)}, u32[]{:S(2)}) collective-permute-start(f32[96,256]{1,0:T(8,128)} %refs_3_.1), channel_id=1, source_target_pairs={{0,15},{1,0},{2,1},{3,2},{4,3},{5,4},{6,5},{7,6},{8,7},{9,8},{10,9... | collective-permute-start | bytes 294920 | tf_op jit(solution)/shard_map/ppermute | solution.py:34
  10.9 0.0 collective-permute-done.refs_0_
  10.9 3.2 %collective-permute-start.4 = (f32[96,256]{1,0:T(8,128)}, f32[96,256]{1,0:T(8,128)S(1)}, u32[]{:S(2)}, u32[]{:S(2)}) collective-permute-start(f32[96,256]{1,0:T(8,128)} %refs_3_.1), channel_id=1, source_target_pairs={{0,14},{1,15},{2,0},{3,1},{4,2},{5,3},{6,4},{7,5},{8,6},{9,7},{10,... | collective-permute-start | bytes 294920 | tf_op jit(solution)/shard_map/ppermute | solution.py:34
  14.0 0.8 %collective-permute-done.1.refs_1_ = f32[96,256]{1,0:T(8,128)S(1)} collective-permute-done((f32[96,256]{1,0:T(8,128)}, f32[96,256]{1,0:T(8,128)S(1)}, u32[]{:S(2)}, u32[]{:S(2)}) %collective-permute-start.1) | collective-permute-done | bytes 98336 | tf_op jit(solution)/shard_map/ppermute | solution.py:34
  14.8 0.6 collective-permute-start.5
  15.4 2.4 %prep_n.2 = (bf16[3072,256]{1,0:T(8,128)(2,1)S(1)}, bf16[3072,256]{1,0:T(8,128)(2,1)S(1)}) custom-call(f32[48,12288]{1,0:T(8,128)} %src.5), custom_call_target="tpu_custom_call" | custom-call | tf_op jit(solution)/shard_map/prep_n/pallas_call | solution.py:127
  18.4 0.0 copy-start
  18.4 0.0 copy-start.1
  18.4 4.1 %prep_t.1 = (bf16[384,6144]{1,0:T(8,128)(2,1)S(1)}, bf16[384,6144]{1,0:T(8,128)(2,1)S(1)}) custom-call(f32[384,6144]{1,0:T(8,128)} %src.4), custom_call_target="tpu_custom_call" | custom-call | tf_op jit(solution)/shard_map/prep_t/pallas_call | solution.py:70
  22.5 0.0 collective-permute-done.2.refs_2_
  22.5 0.0 collective-permute-done.3.refs_4_
  22.5 0.0 collective-permute-done.4.refs_5_
  22.5 0.0 collective-permute-done.5.refs_6_
  22.5 0.0 copy-done
  22.6 0.0 copy-done.1
  22.6 0.7 %select.1.c = bf16[192,384]{1,0:T(8,128)(2,1)S(1)} custom-call(f32[96,256]{1,0:T(8,128)S(1)} %collective-permute-done.refs_0_, f32[96,256]{1,0:T(8,128)S(1)} %collective-permute-done.1.refs_1_, f32[96,256]{1,0:T(8,128)S(1)} %collective-permute-done.2.refs_2_, f32[96,256]{1,0:T(8,128)S(1)} %copy-done, f32[96,256]{1,0:T(8,128)S(1)} %collective-permute-done.3.refs_4_, ...), custom_call_target="tpu_custom_call" | custom-call | tf_op jit(solution)/shard_map/select/pallas_call | solution.py:160
  23.2 1.5 %multiply.2 = (f32[1024,128]{1,0:T(8,128)S(1)}, f32[2048,128]{1,0:T(8,128)S(1)}) custom-call(bf16[192,384]{1,0:T(8,128)(2,1)S(1)} %select.1.c, bf16[384,6144]{1,0:T(8,128)(2,1)S(1)} %get-tuple-element.18.hi, bf16[384,6144]{1,0:T(8,128)(2,1)S(1)} %get-tuple-element.19.lo), custom_call_target="tpu_custom_call" | custom-call | tf_op jit(solution)/shard_map/multiply/pallas_call | solution.py:188
  24.7 0.6 collective-permute-start.11
  25.3 0.8 %multiply.3 = (f32[512,128]{1,0:T(8,128)S(1)}, f32[1024,128]{1,0:T(8,128)S(1)}) custom-call(bf16[192,384]{1,0:T(8,128)(2,1)S(1)} %select.1.c, bf16[384,6144]{1,0:T(8,128)(2,1)S(1)} %get-tuple-element.18.hi, bf16[384,6144]{1,0:T(8,128)(2,1)S(1)} %get-tuple-element.19.lo), custom_call_target="tpu_custom_call" | custom-call | tf_op jit(solution)/shard_map/multiply/pallas_call | solution.py:188
  26.1 1.6 %collective-permute-start.10 = (f32[512,128]{1,0:T(8,128)S(1)}, f32[512,128]{1,0:T(8,128)S(1)}, u32[]{:S(2)}, u32[]{:S(2)}) collective-permute-start(f32[512,128]{1,0:T(8,128)S(1)} %get-tuple-element.27), channel_id=1, source_target_pairs={{0,16},{16,0},{1,17},{17,1},{2,18},{18,2},{3,19},{19,3},{4,20},{20... | collective-permute-start | bytes 786440 | tf_op jit(solution)/shard_map/ppermute | solution.py:295
  27.7 17.0 %collective-permute-done.10.refs_0_ = f32[512,128]{1,0:T(8,128)S(1)} collective-permute-done((f32[512,128]{1,0:T(8,128)S(1)}, f32[512,128]{1,0:T(8,128)S(1)}, u32[]{:S(2)}, u32[]{:S(2)}) %collective-permute-start.10) | collective-permute-done | bytes 262176 | tf_op jit(solution)/shard_map/ppermute | solution.py:295
  44.6 0.7 %contract.4.hr = f32[32,192]{1,0:T(8,128)S(1)} custom-call(f32[512,128]{1,0:T(8,128)S(1)} %collective-permute-done.10.refs_0_, bf16[3072,256]{1,0:T(8,128)(2,1)S(1)} %get-tuple-element.17.refs_9_.refs_2_.refs_1_, bf16[3072,256]{1,0:T(8,128)(2,1)S(1)} %get-tuple-element.22.refs_3_.refs_2_), custom_call_target="tpu_custom_call" | custom-call | tf_op jit(solution)/shard_map/contract/pallas_call | solution.py:248
  45.3 0.6 collective-permute-start.14
  45.9 0.0 collective-permute-done.6.src
  45.9 0.8 %prep_n.3 = (bf16[1024,256]{1,0:T(8,128)(2,1)S(1)}, bf16[1024,256]{1,0:T(8,128)(2,1)S(1)}) custom-call(f32[16,12288]{1,0:T(8,128)S(1)} %collective-permute-done.6.src), custom_call_target="tpu_custom_call" | custom-call | tf_op jit(solution)/shard_map/prep_n/pallas_call | solution.py:127
  46.8 2.4 %contract.3 = (f32[64,192]{1,0:T(8,128)S(1)}, f32[32,192]{1,0:T(8,128)S(1)}) custom-call(f32[2048,128]{1,0:T(8,128)S(1)} %get-tuple-element.20.refs_0_, f32[1024,128]{1,0:T(8,128)S(1)} %get-tuple-element.21.refs_1_, bf16[3072,256]{1,0:T(8,128)(2,1)S(1)} %get-tuple-element.17.refs_9_.refs_2_.refs_1_, bf16[3072,256]{1,0:T(8,128)(2,1)S(1)} %get-tuple-element.22.refs_3_.refs_2_, ...), custom_call_target="tpu_custom_call" | custom-call | tf_op jit(solution)/shard_map/contract/pallas_call | solution.py:248
  49.1 0.0 collective-permute-done.11.refs_0_
  49.1 0.7 %contract.5 = f32[64,192]{1,0:T(8,128)S(1)} custom-call(f32[1024,128]{1,0:T(8,128)S(1)} %collective-permute-done.11.refs_0_, bf16[3072,256]{1,0:T(8,128)(2,1)S(1)} %get-tuple-element.17.refs_9_.refs_2_.refs_1_, bf16[3072,256]{1,0:T(8,128)(2,1)S(1)} %get-tuple-element.22.refs_3_.refs_2_, f32[32,192]{1,0:T(8,128)S(1)} %get-tuple-element.25.refs_3_.ho), custom_call_target="tpu_custom_call" | custom-call | tf_op jit(solution)/shard_map/contract/pallas_call | solution.py:248
  49.9 0.1 collective-permute-start.12
  49.9 1.6 %collective-permute-start.13 = (f32[64,192]{1,0:T(8,128)S(1)}, f32[64,192]{1,0:T(8,128)S(1)}, u32[]{:S(2)}, u32[]{:S(2)}) collective-permute-start(f32[64,192]{1,0:T(8,128)S(1)} %contract.5), channel_id=1, source_target_pairs={{0,17},{1,18},{2,19},{3,20},{4,21},{5,22},{6,23},{7,24},{8,25},{9,... | collective-permute-start | bytes 147464 | tf_op jit(solution)/shard_map/ppermute | solution.py:44
  51.6 4.5 %collective-permute-start.7 = (f32[64,192]{1,0:T(8,128)S(1)}, f32[64,192]{1,0:T(8,128)S(1)}, u32[]{:S(2)}, u32[]{:S(2)}) collective-permute-start(f32[64,192]{1,0:T(8,128)S(1)} %get-tuple-element.26), channel_id=1, source_target_pairs={{0,15},{1,0},{2,1},{3,2},{4,3},{5,4},{6,5},{7,6},{8,7},{9,8},{10,9... | collective-permute-start | bytes 147464 | tf_op jit(solution)/shard_map/ppermute | solution.py:44
  56.1 3.6 %collective-permute-start.8 = (f32[64,192]{1,0:T(8,128)S(1)}, f32[64,192]{1,0:T(8,128)S(1)}, u32[]{:S(2)}, u32[]{:S(2)}) collective-permute-start(f32[64,192]{1,0:T(8,128)S(1)} %get-tuple-element.26), channel_id=1, source_target_pairs={{0,31},{1,16},{2,17},{3,18},{4,19},{5,20},{6,21},{7,22},{8,23},{9,... | collective-permute-start | bytes 147464 | tf_op jit(solution)/shard_map/ppermute | solution.py:44
  59.7 0.0 collective-permute-done.14.rc
  59.7 0.0 collective-permute-start.9
  59.7 4.0 %collective-permute-done.9.oc = f32[32,192]{1,0:T(8,128)S(1)} collective-permute-done((f32[32,192]{1,0:T(8,128)S(1)}, f32[32,192]{1,0:T(8,128)S(1)}, u32[]{:S(2)}, u32[]{:S(2)}) %collective-permute-start.9) | collective-permute-done | bytes 24608 | tf_op jit(solution)/shard_map/ppermute | solution.py:44
  63.7 0.0 collective-permute-done.12.ra
  63.7 0.0 collective-permute-done.13.rb
  63.7 0.0 collective-permute-done.7.oa
  63.8 0.0 collective-permute-done.8.ob
  63.8 0.7 %finish.1 = f32[64,320]{1,0:T(8,128)} custom-call(f32[32,192]{1,0:T(8,128)S(1)} %get-tuple-element.25.refs_3_.ho, f32[64,192]{1,0:T(8,128)S(1)} %collective-permute-done.7.oa, f32[64,192]{1,0:T(8,128)S(1)} %collective-permute-done.8.ob, f32[32,192]{1,0:T(8,128)S(1)} %collective-permute-done.9.oc, f32[32,192]{1,0:T(8,128)S(1)} %contract.4.hr, ...), custom_call_target="tpu_custom_call" | custom-call | tf_op jit(solution)/shard_map/finish/pallas_call | solution.py:268
Async XLA Ops:
  1.1 44.8 %collective-permute-start.6 = (f32[16,12288]{1,0:T(8,128)S(1)}, f32[16,12288]{1,0:T(8,128)S(1)}, u32[]{:S(2)}, u32[]{:S(2)}) collective-permute-start(f32[16,12288]{1,0:T(8,128)S(1)} %head.1), channel_id=1, source_target_pairs={{0,16},{16,0},{1,17},{17,1},{2,18},{18,2},{3,19},{19,3},{4,20},{20... | collective-permute-start | bytes 2359304 | tf_op jit(solution)/shard_map/ppermute | solution.py:285
  4.2 6.6 %collective-permute-start = (f32[96,256]{1,0:T(8,128)}, f32[96,256]{1,0:T(8,128)S(1)}, u32[]{:S(2)}, u32[]{:S(2)}) collective-permute-start(f32[96,256]{1,0:T(8,128)} %refs_3_.1), channel_id=1, source_target_pairs={{0,3},{1,4},{2,5},{3,6},{4,7},{5,8},{6,9},{7,10},{8,11},{9,12},{10... | collective-permute-start | bytes 294920 | tf_op jit(solution)/shard_map/ppermute | solution.py:34
  4.9 9.9 %collective-permute-start.1 = (f32[96,256]{1,0:T(8,128)}, f32[96,256]{1,0:T(8,128)S(1)}, u32[]{:S(2)}, u32[]{:S(2)}) collective-permute-start(f32[96,256]{1,0:T(8,128)} %refs_3_.1), channel_id=1, source_target_pairs={{0,2},{1,3},{2,4},{3,5},{4,6},{5,7},{6,8},{7,9},{8,10},{9,11},{10,... | collective-permute-start | bytes 294920 | tf_op jit(solution)/shard_map/ppermute | solution.py:34
  6.4 16.1 %collective-permute-start.2 = (f32[96,256]{1,0:T(8,128)}, f32[96,256]{1,0:T(8,128)S(1)}, u32[]{:S(2)}, u32[]{:S(2)}) collective-permute-start(f32[96,256]{1,0:T(8,128)} %refs_3_.1), channel_id=1, source_target_pairs={{0,1},{1,2},{2,3},{3,4},{4,5},{5,6},{6,7},{7,8},{8,9},{9,10},{10,1... | collective-permute-start | bytes 294920 | tf_op jit(solution)/shard_map/ppermute | solution.py:34
  7.1 15.4 %collective-permute-start.3 = (f32[96,256]{1,0:T(8,128)}, f32[96,256]{1,0:T(8,128)S(1)}, u32[]{:S(2)}, u32[]{:S(2)}) collective-permute-start(f32[96,256]{1,0:T(8,128)} %refs_3_.1), channel_id=1, source_target_pairs={{0,15},{1,0},{2,1},{3,2},{4,3},{5,4},{6,5},{7,6},{8,7},{9,8},{10,9... | collective-permute-start | bytes 294920 | tf_op jit(solution)/shard_map/ppermute | solution.py:34
  10.9 11.7 %collective-permute-start.4 = (f32[96,256]{1,0:T(8,128)}, f32[96,256]{1,0:T(8,128)S(1)}, u32[]{:S(2)}, u32[]{:S(2)}) collective-permute-start(f32[96,256]{1,0:T(8,128)} %refs_3_.1), channel_id=1, source_target_pairs={{0,14},{1,15},{2,0},{3,1},{4,2},{5,3},{6,4},{7,5},{8,6},{9,7},{10,... | collective-permute-start | bytes 294920 | tf_op jit(solution)/shard_map/ppermute | solution.py:34
  14.8 7.7 %collective-permute-start.5 = (f32[96,256]{1,0:T(8,128)}, f32[96,256]{1,0:T(8,128)S(1)}, u32[]{:S(2)}, u32[]{:S(2)}) collective-permute-start(f32[96,256]{1,0:T(8,128)} %refs_3_.1), channel_id=1, source_target_pairs={{0,13},{1,14},{2,15},{3,0},{4,1},{5,2},{6,3},{7,4},{8,5},{9,6},{10... | collective-permute-start | bytes 294920 | tf_op jit(solution)/shard_map/ppermute | solution.py:34
  18.4 4.1 %copy-start = (f32[96,256]{1,0:T(8,128)S(1)}, f32[96,256]{1,0:T(8,128)}, u32[]{:S(2)}) copy-start(f32[96,256]{1,0:T(8,128)} %refs_3_.1) | copy-start | bytes 294916
  18.4 4.1 %copy-start.1 = (s32[1,1,3]{2,1,0:T(1,128)S(1)}, s32[1,1,3]{2,1,0:T(1,128)}, u32[]{:S(2)}) copy-start(s32[1,1,3]{2,1,0:T(1,128)} %refs_7_.1) | copy-start | bytes 40
  24.7 24.4 %collective-permute-start.11 = (f32[1024,128]{1,0:T(8,128)S(1)}, f32[1024,128]{1,0:T(8,128)S(1)}, u32[]{:S(2)}, u32[]{:S(2)}) collective-permute-start(f32[1024,128]{1,0:T(8,128)S(1)} %get-tuple-element.28), channel_id=1, source_target_pairs={{0,16},{16,0},{1,17},{17,1},{2,18},{18,2},{3,19},{19,3},{4,20},{20... | collective-permute-start | bytes 1572872 | tf_op jit(solution)/shard_map/ppermute | solution.py:293
  26.1 18.5 %collective-permute-start.10 = (f32[512,128]{1,0:T(8,128)S(1)}, f32[512,128]{1,0:T(8,128)S(1)}, u32[]{:S(2)}, u32[]{:S(2)}) collective-permute-start(f32[512,128]{1,0:T(8,128)S(1)} %get-tuple-element.27), channel_id=1, source_target_pairs={{0,16},{16,0},{1,17},{17,1},{2,18},{18,2},{3,19},{19,3},{4,20},{20... | collective-permute-start | bytes 786440 | tf_op jit(solution)/shard_map/ppermute | solution.py:295
  45.3 14.3 %collective-permute-start.14 = (f32[32,192]{1,0:T(8,128)S(1)}, f32[32,192]{1,0:T(8,128)S(1)}, u32[]{:S(2)}, u32[]{:S(2)}) collective-permute-start(f32[32,192]{1,0:T(8,128)S(1)} %contract.4.hr), channel_id=1, source_target_pairs={{0,16},{1,17},{2,18},{3,19},{4,20},{5,21},{6,22},{7,23},{8,24},{9,... | collective-permute-start | bytes 73736 | tf_op jit(solution)/shard_map/ppermute | solution.py:44
  49.9 13.9 %collective-permute-start.12 = (f32[64,192]{1,0:T(8,128)S(1)}, f32[64,192]{1,0:T(8,128)S(1)}, u32[]{:S(2)}, u32[]{:S(2)}) collective-permute-start(f32[64,192]{1,0:T(8,128)S(1)} %contract.5), channel_id=1, source_target_pairs={{0,1},{1,2},{2,3},{3,4},{4,5},{5,6},{6,7},{7,8},{8,9},{9,10},{10,1... | collective-permute-start | bytes 147464 | tf_op jit(solution)/shard_map/ppermute | solution.py:44
  49.9 13.8 %collective-permute-start.13 = (f32[64,192]{1,0:T(8,128)S(1)}, f32[64,192]{1,0:T(8,128)S(1)}, u32[]{:S(2)}, u32[]{:S(2)}) collective-permute-start(f32[64,192]{1,0:T(8,128)S(1)} %contract.5), channel_id=1, source_target_pairs={{0,17},{1,18},{2,19},{3,20},{4,21},{5,22},{6,23},{7,24},{8,25},{9,... | collective-permute-start | bytes 147464 | tf_op jit(solution)/shard_map/ppermute | solution.py:44
  51.6 12.2 %collective-permute-start.7 = (f32[64,192]{1,0:T(8,128)S(1)}, f32[64,192]{1,0:T(8,128)S(1)}, u32[]{:S(2)}, u32[]{:S(2)}) collective-permute-start(f32[64,192]{1,0:T(8,128)S(1)} %get-tuple-element.26), channel_id=1, source_target_pairs={{0,15},{1,0},{2,1},{3,2},{4,3},{5,4},{6,5},{7,6},{8,7},{9,8},{10,9... | collective-permute-start | bytes 147464 | tf_op jit(solution)/shard_map/ppermute | solution.py:44
  56.1 7.7 %collective-permute-start.8 = (f32[64,192]{1,0:T(8,128)S(1)}, f32[64,192]{1,0:T(8,128)S(1)}, u32[]{:S(2)}, u32[]{:S(2)}) collective-permute-start(f32[64,192]{1,0:T(8,128)S(1)} %get-tuple-element.26), channel_id=1, source_target_pairs={{0,31},{1,16},{2,17},{3,18},{4,19},{5,20},{6,21},{7,22},{8,23},{9,... | collective-permute-start | bytes 147464 | tf_op jit(solution)/shard_map/ppermute | solution.py:44
  59.7 4.0 %collective-permute-start.9 = (f32[32,192]{1,0:T(8,128)S(1)}, f32[32,192]{1,0:T(8,128)S(1)}, u32[]{:S(2)}, u32[]{:S(2)}) collective-permute-start(f32[32,192]{1,0:T(8,128)S(1)} %get-tuple-element.25.refs_3_.ho), channel_id=1, source_target_pairs={{0,16},{1,17},{2,18},{3,19},{4,20},{5,21},{6,22},{7,23},{8,24},{9,... | collective-permute-start | bytes 73736 | tf_op jit(solution)/shard_map/ppermute | solution.py:44
where the time goes:
time: 64.7 us; the launch traced here: 64.5 us
  starting transfers between devices  26 us (40%)
  waiting for transfers between devices  21.8 us (34%)
  Pallas kernels  15.9 us (25%)
  between operations  0.82 us (1%)
    ppermute x1, waiting for transfers between devices, paired(): far_rest = lax.ppermute(far_rest, 'tens', swap)  17 us
    ppermute x6, starting transfers between devices, shift(): lax.ppermute(x, 'atom', [(i, (i + by) % atoms) for i in range(atoms)])  10.4 us
    ppermute x6, starting transfers between devices, send(): return lax.ppermute(x, ('tens', 'atom'), pairs)  10.4 us
    pallas_call x1, Pallas kernels, prep_t(): pl.pallas_call(body, in_specs=[HB], out_specs=[VM, VM], out_shape=[vmem((...  4.05 us
    ppermute x6, waiting for transfers between devices, send(): return lax.ppermute(x, ('tens', 'atom'), pairs)  4.05 us
    pallas_call x3, Pallas kernels, contract(): pl.pallas_call(body, in_specs=[VM] * (len(stretches) + len(flat) + len(af...  3.77 us
    pallas_call x2, Pallas kernels, prep_n(): pl.pallas_call(body, in_specs=[HB], out_specs=[VM, VM], out_shape=[vmem((...  3.21 us
    ppermute x1, starting transfers between devices, paired(): n_far = lax.ppermute(head(n_saved, early), 'tens', swap)  3.06 us
  transfers between devices with their start and end apart: 15, of which 3 were waited for; matrix products, arithmetic and copies ran while one was open for 0% of the time, Pallas kernels for 22%

commit v1 on v0

--- a/solution.py
+++ b/solution.py
@@ -9,8 +9,8 @@
 LANES = 128
 SUBL = 8
 REACH = 3
+ORDER = (-3, -2, -1, 3, 2, 1)
 VM = pl.BlockSpec(memory_space=pltpu.VMEM)
-SM = pl.BlockSpec(memory_space=pltpu.SMEM)
 HB = pl.BlockSpec(memory_space=pltpu.HBM)
 f32 = jnp.float32
 bf16 = jnp.bfloat16
@@ -44,34 +44,36 @@
     return lax.ppermute(x, ("tens", "atom"), pairs)
 
 
-def prep_t(t_blocks):
-    rows, cols = t_blocks.shape
+def prep_t(t_blocks, first, slope, cols):
+    rows = t_blocks.shape[0]
     step = 64
+    sub = 512 if cols % 512 == 0 else LANES
 
     def body(src, hi, lo, buf, sems):
+        start = pl.multiple_of(first + slope * lax.axis_index("tens"), LANES)
         copies = []
         for i in range(rows // step):
             here = pl.ds(i * step, step)
-            copies.append(pltpu.make_async_copy(src.at[here], buf.at[here], sems.at[i]))
+            copies.append(pltpu.make_async_copy(src.at[here, pl.ds(start, cols)], buf.at[here], sems.at[i]))
             copies[-1].start()
         for i in range(rows // step):
             copies[i].wait()
 
             def tile(c, carry, i=i):
-                at = pl.ds(pl.multiple_of(c * 512, 512), 512)
+                at = pl.ds(pl.multiple_of(c * sub, sub), sub)
                 here = pl.ds(i * step, step)
                 h, l = split(buf[here, at])
                 hi[here, at] = h
                 lo[here, at] = l
                 return carry
 
-            lax.fori_loop(0, cols // 512, tile, 0)
+            lax.fori_loop(0, cols // sub, tile, 0)
 
     return pl.pallas_call(
         body, in_specs=[HB], out_specs=[VM, VM],
         out_shape=[vmem((rows, cols), bf16), vmem((rows, cols), bf16)],
         scratch_shapes=[pltpu.VMEM((rows, cols), f32), pltpu.SemaphoreType.DMA((rows // step,))],
-        name="prep_t", compiler_params=limit(14),
+        name="prep_t", compiler_params=limit(12),
     )(t_blocks)
 
 
@@ -133,21 +135,22 @@
     )(saved)
 
 
-def select(pieces, q_list, q_count, p_rows, early, after):
+def select(pieces, q_list, q_count, p_rows, early):
     p_all, width = pieces[0].shape
     ql = q_list.shape[-1]
     blk = LANES
     qb = width // blk
 
     def body(*refs):
-        parts, (ql_ref, qc_ref, _, out, scr) = refs[:len(pieces)], refs[len(pieces):]
+        parts, (list_ref, count_ref, out, scr) = refs[:len(pieces)], refs[len(pieces):]
         t = lax.axis_index("tens")
         for q in range(ql):
-            want = ql_ref[0, 0, q]
-            pick = parts[0][:, :blk]
-            for i in range(1, len(parts) * qb):
+            used = jnp.where(count_ref[...] > q, list_ref[0][:, q:q + 1], -1)
+            want = jnp.broadcast_to(used, (1, blk))
+            pick = jnp.zeros((p_all, blk), f32)
+            for i in range(len(parts) * qb):
                 pick = jnp.where(want == i, parts[i // qb][:, (i % qb) * blk:(i % qb + 1) * blk], pick)
-            scr[:, q * blk:(q + 1) * blk] = jnp.where(q < qc_ref[0, 0], pick, 0.0)
+            scr[:, q * blk:(q + 1) * blk] = pick
         other = (1 - t) * p_rows
         order = ((other + early, p_rows - early), (t * p_rows, p_rows), (other, early))
         at = 0
@@ -158,22 +161,22 @@
             at += size
 
     return pl.pallas_call(
-        body, in_specs=[VM] * len(pieces) + [SM, SM, VM], out_specs=VM,
+        body, in_specs=[VM] * (len(pieces) + 2), out_specs=VM,
         out_shape=vmem((2 * p_all, ql * blk), bf16),
         scratch_shapes=[pltpu.VMEM((p_all, ql * blk), f32)], name="select", compiler_params=limit(8),
-    )(*pieces, q_list, q_count, after)
-
-
-def multiply(chosen, t_hi, t_lo, first, slope, cols, cross):
+    )(*pieces, q_list, q_count)
+
+
+def multiply(chosen, t_parts, cross):
     p_all = chosen.shape[0] // 2
+    cols = t_parts[0].shape[1]
     own = p_all - cross
     ct = cols // LANES
     sub = 512 if cols % 512 == 0 else 256
 
     def body(c, hi, lo, out_c, out_o):
-        start = first + slope * lax.axis_index("tens")
         for j in range(cols // sub):
-            at = pl.ds(pl.multiple_of(start + j * sub, LANES), sub)
+            at = pl.ds(j * sub, sub)
             big = jnp.dot(c[...], hi[:, at], preferred_element_type=f32)
             val = big[:p_all] + big[p_all:] + jnp.dot(c[:p_all, :], lo[:, at], preferred_element_type=f32)
             for k in range(sub // LANES):
@@ -188,7 +191,7 @@
     return pl.pallas_call(
         body, in_specs=[VM] * 3, out_specs=[VM, VM],
         out_shape=[vmem((cross * ct, LANES), f32), vmem((own * ct, LANES), f32)], name="multiply", compiler_params=limit(8),
-    )(chosen, t_hi, t_lo)
+    )(chosen, *t_parts)
 
 
 def contract_into(x, rows, ct, n_parts, n_rows, l_hi, l_lo):
@@ -283,17 +286,18 @@
     n_saved = pltpu.with_memory_space_constraint(n_saved, pltpu.HBM)
     t_blocks = pltpu.with_memory_space_constraint(t_blocks, pltpu.HBM)
     n_far = lax.ppermute(head(n_saved, early), "tens", swap)
-    pieces = [chibar if o == 0 else shift(chibar, -o) for o in range(-REACH, REACH + 1)]
-    t_hi, t_lo = prep_t(t_blocks)
+    moved = {o: shift(chibar, -o) for o in ORDER}
+    pieces = [moved[o] if o else chibar for o in range(-REACH, REACH + 1)]
+    rest = nu_t - orb
+    t_main = prep_t(t_blocks, 0, rest * orb, orb * orb)
+    chosen = select(pieces, q_list, q_count, p_rows, early)
+    far_main, own_main = multiply(chosen, t_main, cross)
+    far_main = lax.ppermute(far_main, "tens", swap)
+    t_rest = prep_t(t_blocks, orb * orb, -orb * orb, rest * orb)
+    far_rest, own_rest = multiply(chosen, t_rest, cross)
+    far_rest = lax.ppermute(far_rest, "tens", swap)
+
     near = prep_n(n_saved, orb)
-    chosen = select(pieces, q_list, q_count, p_rows, early, near[0])
-
-    rest = nu_t - orb
-    far_main, own_main = multiply(chosen, t_hi, t_lo, 0, rest * orb, orb * orb, cross)
-    far_main = lax.ppermute(far_main, "tens", swap)
-    far_rest, own_rest = multiply(chosen, t_hi, t_lo, orb * orb, -orb * orb, rest * orb, cross)
-    far_rest = lax.ppermute(far_rest, "tens", swap)
-
     beyond = prep_n(n_far, orb)
     o_main, o_rest = contract([own_main, own_rest], p_rows + early, [near, beyond], [(0, p_rows), (0, early)],
                               band, [orb, rest])

time: 64.7 us -> 60.8 us (0.940)
  waiting for transfers between devices: 21.8 us -> 17.6 us
    ppermute x1, waiting for transfers between devices: 17 us -> 12.3 us  [paired(): far_rest = lax.ppermute(far_rest, 'tens', swap)]
    pallas_call x1 -> x2, Pallas kernels: 4.05 us -> 4.96 us  [prep_t(): pl.pallas_call(body, in_specs=[HB], out_specs=[VM, VM], out_shape=[vmem((...]
  transfers between devices with their start and end apart: 15 -> 15, of which waited for: 3 -> 4; matrix products, arithmetic and copies ran while one was open for 0% -> 0% of each run, Pallas kernels for 22% -> 24%
where the time goes in v1:
time: 60.8 us; the launch traced here: 60.6 us
  starting transfers between devices  25.8 us (42%)
  waiting for transfers between devices  17.6 us (29%)
  Pallas kernels  16.4 us (27%)
  between operations  0.8 us (1%)
    ppermute x1, waiting for transfers between devices, paired(): far_rest = lax.ppermute(far_rest, 'tens', swap)  12.3 us
    ppermute x6, starting transfers between devices, send(): return lax.ppermute(x, ('tens', 'atom'), pairs)  10.4 us
    ppermute x6, starting transfers between devices, shift(): lax.ppermute(x, 'atom', [(i, (i + by) % atoms) for i in range(atoms)])  10.2 us
    pallas_call x2, Pallas kernels, prep_t(): pl.pallas_call(body, in_specs=[HB], out_specs=[VM, VM], out_shape=[vmem((...  4.96 us
    ppermute x6, waiting for transfers between devices, send(): return lax.ppermute(x, ('tens', 'atom'), pairs)  4.19 us
    pallas_call x3, Pallas kernels, contract(): pl.pallas_call(body, in_specs=[VM] * (len(stretches) + len(flat) + len(af...  3.78 us
    pallas_call x2, Pallas kernels, prep_n(): pl.pallas_call(body, in_specs=[HB], out_specs=[VM, VM], out_shape=[vmem((...  3.21 us
    ppermute x1, starting transfers between devices, paired(): n_far = lax.ppermute(head(n_saved, early), 'tens', swap)  3.06 us
  transfers between devices with their start and end apart: 15, of which 4 were waited for; matrix products, arithmetic and copies ran while one was open for 0% of the time, Pallas kernels for 24%

profile of v1, /device:TPU:0, one launch (start us, length us, event | category | flops | bytes accessed | tf_op | source)
XLA Modules:
  0.0 60.6 jit_solution(10990322929449707652)
XLA Ops:
  0.0 0.0 copy-start
  0.0 1.2 %head.1 = f32[16,12288]{1,0:T(8,128)S(1)} custom-call(f32[48,12288]{1,0:T(8,128)} %src.7), custom_call_target="tpu_custom_call" | custom-call | tf_op jit(solution)/shard_map/head/pallas_call | solution.py:86
  1.2 0.0 copy-start.1
  1.2 3.1 %collective-permute-start.6 = (f32[16,12288]{1,0:T(8,128)S(1)}, f32[16,12288]{1,0:T(8,128)S(1)}, u32[]{:S(2)}, u32[]{:S(2)}) collective-permute-start(f32[16,12288]{1,0:T(8,128)S(1)} %head.1), channel_id=1, source_target_pairs={{0,16},{16,0},{1,17},{17,1},{2,18},{18,2},{3,19},{19,3},{4,20},{20... | collective-permute-start | bytes 2359304 | tf_op jit(solution)/shard_map/ppermute | solution.py:288
  4.3 0.0 copy-done
  4.3 0.7 %collective-permute-start = (f32[96,256]{1,0:T(8,128)S(1)}, f32[96,256]{1,0:T(8,128)S(1)}, u32[]{:S(2)}, u32[]{:S(2)}) collective-permute-start(f32[96,256]{1,0:T(8,128)S(1)} %copy-done), channel_id=1, source_target_pairs={{0,3},{1,4},{2,5},{3,6},{4,7},{5,8},{6,9},{7,10},{8,11},{9,12},{10... | collective-permute-start | bytes 294920 | tf_op jit(solution)/shard_map/ppermute | solution.py:34
  4.9 1.5 %collective-permute-start.1 = (f32[96,256]{1,0:T(8,128)S(1)}, f32[96,256]{1,0:T(8,128)S(1)}, u32[]{:S(2)}, u32[]{:S(2)}) collective-permute-start(f32[96,256]{1,0:T(8,128)S(1)} %copy-done), channel_id=1, source_target_pairs={{0,2},{1,3},{2,4},{3,5},{4,6},{5,7},{6,8},{7,9},{8,10},{9,11},{10,... | collective-permute-start | bytes 294920 | tf_op jit(solution)/shard_map/ppermute | solution.py:34
  6.5 0.7 %collective-permute-start.2 = (f32[96,256]{1,0:T(8,128)S(1)}, f32[96,256]{1,0:T(8,128)S(1)}, u32[]{:S(2)}, u32[]{:S(2)}) collective-permute-start(f32[96,256]{1,0:T(8,128)S(1)} %copy-done), channel_id=1, source_target_pairs={{0,1},{1,2},{2,3},{3,4},{4,5},{5,6},{6,7},{7,8},{8,9},{9,10},{10,1... | collective-permute-start | bytes 294920 | tf_op jit(solution)/shard_map/ppermute | solution.py:34
  7.2 3.7 %collective-permute-start.3 = (f32[96,256]{1,0:T(8,128)S(1)}, f32[96,256]{1,0:T(8,128)S(1)}, u32[]{:S(2)}, u32[]{:S(2)}) collective-permute-start(f32[96,256]{1,0:T(8,128)S(1)} %copy-done), channel_id=1, source_target_pairs={{0,15},{1,0},{2,1},{3,2},{4,3},{5,4},{6,5},{7,6},{8,7},{9,8},{10,9... | collective-permute-start | bytes 294920 | tf_op jit(solution)/shard_map/ppermute | solution.py:34
  10.9 0.0 collective-permute-done.refs_0_
  10.9 3.0 %collective-permute-start.4 = (f32[96,256]{1,0:T(8,128)S(1)}, f32[96,256]{1,0:T(8,128)S(1)}, u32[]{:S(2)}, u32[]{:S(2)}) collective-permute-start(f32[96,256]{1,0:T(8,128)S(1)} %copy-done), channel_id=1, source_target_pairs={{0,14},{1,15},{2,0},{3,1},{4,2},{5,3},{6,4},{7,5},{8,6},{9,7},{10,... | collective-permute-start | bytes 294920 | tf_op jit(solution)/shard_map/ppermute | solution.py:34
  13.9 0.8 %collective-permute-done.1.refs_1_ = f32[96,256]{1,0:T(8,128)S(1)} collective-permute-done((f32[96,256]{1,0:T(8,128)S(1)}, f32[96,256]{1,0:T(8,128)S(1)}, u32[]{:S(2)}, u32[]{:S(2)}) %collective-permute-start.1) | collective-permute-done | bytes 98336 | tf_op jit(solution)/shard_map/ppermute | solution.py:34
  14.6 0.6 collective-permute-start.5
  15.2 3.0 %prep_t.2 = (bf16[384,4096]{1,0:T(8,128)(2,1)S(1)}, bf16[384,4096]{1,0:T(8,128)(2,1)S(1)}) custom-call(f32[384,6144]{1,0:T(8,128)} %src.5), custom_call_target="tpu_custom_call" | custom-call | tf_op jit(solution)/shard_map/prep_t/pallas_call | solution.py:72
  18.9 0.0 collective-permute-done.2.refs_2_
  18.9 0.0 collective-permute-done.3.refs_4_
  18.9 0.0 collective-permute-done.4.refs_5_
  18.9 0.3 collective-permute-done.5.refs_6_
  19.2 0.0 copy-done.1
  19.2 0.2 select.1.c
  19.4 1.5 %multiply.2 = (f32[1024,128]{1,0:T(8,128)S(1)}, f32[2048,128]{1,0:T(8,128)S(1)}) custom-call(bf16[192,384]{1,0:T(8,128)(2,1)S(1)} %select.1.c, bf16[384,4096]{1,0:T(8,128)(2,1)S(1)} %get-tuple-element.19.hi, bf16[384,4096]{1,0:T(8,128)(2,1)S(1)} %get-tuple-element.20.lo), custom_call_target="tpu_custom_call" | custom-call | tf_op jit(solution)/shard_map/multiply/pallas_call | solution.py:191
  20.9 0.6 collective-permute-start.11
  21.5 2.0 %prep_t.3 = (bf16[384,2048]{1,0:T(8,128)(2,1)S(1)}, bf16[384,2048]{1,0:T(8,128)(2,1)S(1)}) custom-call(f32[384,6144]{1,0:T(8,128)} %src.5), custom_call_target="tpu_custom_call" | custom-call | tf_op jit(solution)/shard_map/prep_t/pallas_call | solution.py:72
  23.5 0.8 %multiply.3 = (f32[512,128]{1,0:T(8,128)S(1)}, f32[1024,128]{1,0:T(8,128)S(1)}) custom-call(bf16[192,384]{1,0:T(8,128)(2,1)S(1)} %select.1.c, bf16[384,2048]{1,0:T(8,128)(2,1)S(1)} %get-tuple-element.22.hi, bf16[384,2048]{1,0:T(8,128)(2,1)S(1)} %get-tuple-element.23.lo), custom_call_target="tpu_custom_call" | custom-call | tf_op jit(solution)/shard_map/multiply/pallas_call | solution.py:191
  24.3 1.6 %collective-permute-start.10 = (f32[512,128]{1,0:T(8,128)S(1)}, f32[512,128]{1,0:T(8,128)S(1)}, u32[]{:S(2)}, u32[]{:S(2)}) collective-permute-start(f32[512,128]{1,0:T(8,128)S(1)} %get-tuple-element.31), channel_id=1, source_target_pairs={{0,16},{16,0},{1,17},{17,1},{2,18},{18,2},{3,19},{19,3},{4,20},{20... | collective-permute-start | bytes 786440 | tf_op jit(solution)/shard_map/ppermute | solution.py:298
  25.9 2.4 %prep_n.2 = (bf16[3072,256]{1,0:T(8,128)(2,1)S(1)}, bf16[3072,256]{1,0:T(8,128)(2,1)S(1)}) custom-call(f32[48,12288]{1,0:T(8,128)} %src.7), custom_call_target="tpu_custom_call" | custom-call | tf_op jit(solution)/shard_map/prep_n/pallas_call | solution.py:129
  28.2 12.3 %collective-permute-done.10.refs_0_ = f32[512,128]{1,0:T(8,128)S(1)} collective-permute-done((f32[512,128]{1,0:T(8,128)S(1)}, f32[512,128]{1,0:T(8,128)S(1)}, u32[]{:S(2)}, u32[]{:S(2)}) %collective-permute-start.10) | collective-permute-done | bytes 262176 | tf_op jit(solution)/shard_map/ppermute | solution.py:298
  40.6 0.7 %contract.4.hr = f32[32,192]{1,0:T(8,128)S(1)} custom-call(f32[512,128]{1,0:T(8,128)S(1)} %collective-permute-done.10.refs_0_, bf16[3072,256]{1,0:T(8,128)(2,1)S(1)} %get-tuple-element.25.refs_2_.refs_1_, bf16[3072,256]{1,0:T(8,128)(2,1)S(1)} %get-tuple-element.26.refs_3_.refs_2_), custom_call_target="tpu_custom_call" | custom-call | tf_op jit(solution)/shard_map/contract/pallas_call | solution.py:251
  41.3 0.6 collective-permute-start.14
  41.8 0.0 collective-permute-done.6.src
  41.9 0.8 %prep_n.3 = (bf16[1024,256]{1,0:T(8,128)(2,1)S(1)}, bf16[1024,256]{1,0:T(8,128)(2,1)S(1)}) custom-call(f32[16,12288]{1,0:T(8,128)S(1)} %collective-permute-done.6.src), custom_call_target="tpu_custom_call" | custom-call | tf_op jit(solution)/shard_map/prep_n/pallas_call | solution.py:129
  42.7 2.4 %contract.3 = (f32[64,192]{1,0:T(8,128)S(1)}, f32[32,192]{1,0:T(8,128)S(1)}) custom-call(f32[2048,128]{1,0:T(8,128)S(1)} %get-tuple-element.21.refs_0_, f32[1024,128]{1,0:T(8,128)S(1)} %get-tuple-element.24.refs_1_, bf16[3072,256]{1,0:T(8,128)(2,1)S(1)} %get-tuple-element.25.refs_2_.refs_1_, bf16[3072,256]{1,0:T(8,128)(2,1)S(1)} %get-tuple-element.26.refs_3_.refs_2_, ...), custom_call_target="tpu_custom_call" | custom-call | tf_op jit(solution)/shard_map/contract/pallas_call | solution.py:251
  45.1 0.0 collective-permute-done.11.refs_0_
  45.1 0.7 %contract.5 = f32[64,192]{1,0:T(8,128)S(1)} custom-call(f32[1024,128]{1,0:T(8,128)S(1)} %collective-permute-done.11.refs_0_, bf16[3072,256]{1,0:T(8,128)(2,1)S(1)} %get-tuple-element.25.refs_2_.refs_1_, bf16[3072,256]{1,0:T(8,128)(2,1)S(1)} %get-tuple-element.26.refs_3_.refs_2_, f32[32,192]{1,0:T(8,128)S(1)} %get-tuple-element.29.refs_3_.ho), custom_call_target="tpu_custom_call" | custom-call | tf_op jit(solution)/shard_map/contract/pallas_call | solution.py:251
  45.8 0.1 collective-permute-start.12
  45.9 1.6 %collective-permute-start.13 = (f32[64,192]{1,0:T(8,128)S(1)}, f32[64,192]{1,0:T(8,128)S(1)}, u32[]{:S(2)}, u32[]{:S(2)}) collective-permute-start(f32[64,192]{1,0:T(8,128)S(1)} %contract.5), channel_id=1, source_target_pairs={{0,17},{1,18},{2,19},{3,20},{4,21},{5,22},{6,23},{7,24},{8,25},{9,... | collective-permute-start | bytes 147464 | tf_op jit(solution)/shard_map/ppermute | solution.py:44
  47.5 4.7 %collective-permute-start.7 = (f32[64,192]{1,0:T(8,128)S(1)}, f32[64,192]{1,0:T(8,128)S(1)}, u32[]{:S(2)}, u32[]{:S(2)}) collective-permute-start(f32[64,192]{1,0:T(8,128)S(1)} %get-tuple-element.30), channel_id=1, source_target_pairs={{0,15},{1,0},{2,1},{3,2},{4,3},{5,4},{6,5},{7,6},{8,7},{9,8},{10,9... | collective-permute-start | bytes 147464 | tf_op jit(solution)/shard_map/ppermute | solution.py:44
  52.2 3.5 %collective-permute-start.8 = (f32[64,192]{1,0:T(8,128)S(1)}, f32[64,192]{1,0:T(8,128)S(1)}, u32[]{:S(2)}, u32[]{:S(2)}) collective-permute-start(f32[64,192]{1,0:T(8,128)S(1)} %get-tuple-element.30), channel_id=1, source_target_pairs={{0,31},{1,16},{2,17},{3,18},{4,19},{5,20},{6,21},{7,22},{8,23},{9,... | collective-permute-start | bytes 147464 | tf_op jit(solution)/shard_map/ppermute | solution.py:44
  55.6 0.0 collective-permute-done.14.rc
  55.6 0.0 collective-permute-start.9
  55.6 4.2 %collective-permute-done.9.oc = f32[32,192]{1,0:T(8,128)S(1)} collective-permute-done((f32[32,192]{1,0:T(8,128)S(1)}, f32[32,192]{1,0:T(8,128)S(1)}, u32[]{:S(2)}, u32[]{:S(2)}) %collective-permute-start.9) | collective-permute-done | bytes 24608 | tf_op jit(solution)/shard_map/ppermute | solution.py:44
  59.8 0.0 collective-permute-done.12.ra
  59.8 0.0 collective-permute-done.13.rb
  59.8 0.0 collective-permute-done.7.oa
  59.8 0.0 collective-permute-done.8.ob
  59.8 0.7 %finish.1 = f32[64,320]{1,0:T(8,128)} custom-call(f32[32,192]{1,0:T(8,128)S(1)} %get-tuple-element.29.refs_3_.ho, f32[64,192]{1,0:T(8,128)S(1)} %collective-permute-done.7.oa, f32[64,192]{1,0:T(8,128)S(1)} %collective-permute-done.8.ob, f32[32,192]{1,0:T(8,128)S(1)} %collective-permute-done.9.oc, f32[32,192]{1,0:T(8,128)S(1)} %contract.4.hr, ...), custom_call_target="tpu_custom_call" | custom-call | tf_op jit(solution)/shard_map/finish/pallas_call | solution.py:271
Async XLA Ops:
  0.0 4.3 %copy-start = (f32[96,256]{1,0:T(8,128)S(1)}, f32[96,256]{1,0:T(8,128)}, u32[]{:S(2)}) copy-start(f32[96,256]{1,0:T(8,128)} %refs_3_.1) | copy-start | bytes 294916
  1.2 18.0 %copy-start.1 = (s32[1,1,3]{2,1,0:T(1,128)S(1)}, s32[1,1,3]{2,1,0:T(1,128)}, u32[]{:S(2)}) copy-start(s32[1,1,3]{2,1,0:T(1,128)} %refs_7_.1) | copy-start | bytes 40
  1.2 40.7 %collective-permute-start.6 = (f32[16,12288]{1,0:T(8,128)S(1)}, f32[16,12288]{1,0:T(8,128)S(1)}, u32[]{:S(2)}, u32[]{:S(2)}) collective-permute-start(f32[16,12288]{1,0:T(8,128)S(1)} %head.1), channel_id=1, source_target_pairs={{0,16},{16,0},{1,17},{17,1},{2,18},{18,2},{3,19},{19,3},{4,20},{20... | collective-permute-start | bytes 2359304 | tf_op jit(solution)/shard_map/ppermute | solution.py:288
  4.3 6.6 %collective-permute-start = (f32[96,256]{1,0:T(8,128)S(1)}, f32[96,256]{1,0:T(8,128)S(1)}, u32[]{:S(2)}, u32[]{:S(2)}) collective-permute-start(f32[96,256]{1,0:T(8,128)S(1)} %copy-done), channel_id=1, source_target_pairs={{0,3},{1,4},{2,5},{3,6},{4,7},{5,8},{6,9},{7,10},{8,11},{9,12},{10... | collective-permute-start | bytes 294920 | tf_op jit(solution)/shard_map/ppermute | solution.py:34
  4.9 9.7 %collective-permute-start.1 = (f32[96,256]{1,0:T(8,128)S(1)}, f32[96,256]{1,0:T(8,128)S(1)}, u32[]{:S(2)}, u32[]{:S(2)}) collective-permute-start(f32[96,256]{1,0:T(8,128)S(1)} %copy-done), channel_id=1, source_target_pairs={{0,2},{1,3},{2,4},{3,5},{4,6},{5,7},{6,8},{7,9},{8,10},{9,11},{10,... | collective-permute-start | bytes 294920 | tf_op jit(solution)/shard_map/ppermute | solution.py:34
  6.5 12.4 %collective-permute-start.2 = (f32[96,256]{1,0:T(8,128)S(1)}, f32[96,256]{1,0:T(8,128)S(1)}, u32[]{:S(2)}, u32[]{:S(2)}) collective-permute-start(f32[96,256]{1,0:T(8,128)S(1)} %copy-done), channel_id=1, source_target_pairs={{0,1},{1,2},{2,3},{3,4},{4,5},{5,6},{6,7},{7,8},{8,9},{9,10},{10,1... | collective-permute-start | bytes 294920 | tf_op jit(solution)/shard_map/ppermute | solution.py:34
  7.2 11.7 %collective-permute-start.3 = (f32[96,256]{1,0:T(8,128)S(1)}, f32[96,256]{1,0:T(8,128)S(1)}, u32[]{:S(2)}, u32[]{:S(2)}) collective-permute-start(f32[96,256]{1,0:T(8,128)S(1)} %copy-done), channel_id=1, source_target_pairs={{0,15},{1,0},{2,1},{3,2},{4,3},{5,4},{6,5},{7,6},{8,7},{9,8},{10,9... | collective-permute-start | bytes 294920 | tf_op jit(solution)/shard_map/ppermute | solution.py:34
  10.9 8.0 %collective-permute-start.4 = (f32[96,256]{1,0:T(8,128)S(1)}, f32[96,256]{1,0:T(8,128)S(1)}, u32[]{:S(2)}, u32[]{:S(2)}) collective-permute-start(f32[96,256]{1,0:T(8,128)S(1)} %copy-done), channel_id=1, source_target_pairs={{0,14},{1,15},{2,0},{3,1},{4,2},{5,3},{6,4},{7,5},{8,6},{9,7},{10,... | collective-permute-start | bytes 294920 | tf_op jit(solution)/shard_map/ppermute | solution.py:34
  14.6 4.6 %collective-permute-start.5 = (f32[96,256]{1,0:T(8,128)S(1)}, f32[96,256]{1,0:T(8,128)S(1)}, u32[]{:S(2)}, u32[]{:S(2)}) collective-permute-start(f32[96,256]{1,0:T(8,128)S(1)} %copy-done), channel_id=1, source_target_pairs={{0,13},{1,14},{2,15},{3,0},{4,1},{5,2},{6,3},{7,4},{8,5},{9,6},{10... | collective-permute-start | bytes 294920 | tf_op jit(solution)/shard_map/ppermute | solution.py:34
  20.9 24.2 %collective-permute-start.11 = (f32[1024,128]{1,0:T(8,128)S(1)}, f32[1024,128]{1,0:T(8,128)S(1)}, u32[]{:S(2)}, u32[]{:S(2)}) collective-permute-start(f32[1024,128]{1,0:T(8,128)S(1)} %get-tuple-element.32), channel_id=1, source_target_pairs={{0,16},{16,0},{1,17},{17,1},{2,18},{18,2},{3,19},{19,3},{4,20},{20... | collective-permute-start | bytes 1572872 | tf_op jit(solution)/shard_map/ppermute | solution.py:295
  24.3 16.3 %collective-permute-start.10 = (f32[512,128]{1,0:T(8,128)S(1)}, f32[512,128]{1,0:T(8,128)S(1)}, u32[]{:S(2)}, u32[]{:S(2)}) collective-permute-start(f32[512,128]{1,0:T(8,128)S(1)} %get-tuple-element.31), channel_id=1, source_target_pairs={{0,16},{16,0},{1,17},{17,1},{2,18},{18,2},{3,19},{19,3},{4,20},{20... | collective-permute-start | bytes 786440 | tf_op jit(solution)/shard_map/ppermute | solution.py:298
  41.3 14.4 %collective-permute-start.14 = (f32[32,192]{1,0:T(8,128)S(1)}, f32[32,192]{1,0:T(8,128)S(1)}, u32[]{:S(2)}, u32[]{:S(2)}) collective-permute-start(f32[32,192]{1,0:T(8,128)S(1)} %contract.4.hr), channel_id=1, source_target_pairs={{0,16},{1,17},{2,18},{3,19},{4,20},{5,21},{6,22},{7,23},{8,24},{9,... | collective-permute-start | bytes 73736 | tf_op jit(solution)/shard_map/ppermute | solution.py:44
  45.8 14.0 %collective-permute-start.12 = (f32[64,192]{1,0:T(8,128)S(1)}, f32[64,192]{1,0:T(8,128)S(1)}, u32[]{:S(2)}, u32[]{:S(2)}) collective-permute-start(f32[64,192]{1,0:T(8,128)S(1)} %contract.5), channel_id=1, source_target_pairs={{0,1},{1,2},{2,3},{3,4},{4,5},{5,6},{6,7},{7,8},{8,9},{9,10},{10,1... | collective-permute-start | bytes 147464 | tf_op jit(solution)/shard_map/ppermute | solution.py:44
  45.9 14.0 %collective-permute-start.13 = (f32[64,192]{1,0:T(8,128)S(1)}, f32[64,192]{1,0:T(8,128)S(1)}, u32[]{:S(2)}, u32[]{:S(2)}) collective-permute-start(f32[64,192]{1,0:T(8,128)S(1)} %contract.5), channel_id=1, source_target_pairs={{0,17},{1,18},{2,19},{3,20},{4,21},{5,22},{6,23},{7,24},{8,25},{9,... | collective-permute-start | bytes 147464 | tf_op jit(solution)/shard_map/ppermute | solution.py:44
  47.5 12.3 %collective-permute-start.7 = (f32[64,192]{1,0:T(8,128)S(1)}, f32[64,192]{1,0:T(8,128)S(1)}, u32[]{:S(2)}, u32[]{:S(2)}) collective-permute-start(f32[64,192]{1,0:T(8,128)S(1)} %get-tuple-element.30), channel_id=1, source_target_pairs={{0,15},{1,0},{2,1},{3,2},{4,3},{5,4},{6,5},{7,6},{8,7},{9,8},{10,9... | collective-permute-start | bytes 147464 | tf_op jit(solution)/shard_map/ppermute | solution.py:44
  52.2 7.7 %collective-permute-start.8 = (f32[64,192]{1,0:T(8,128)S(1)}, f32[64,192]{1,0:T(8,128)S(1)}, u32[]{:S(2)}, u32[]{:S(2)}) collective-permute-start(f32[64,192]{1,0:T(8,128)S(1)} %get-tuple-element.30), channel_id=1, source_target_pairs={{0,31},{1,16},{2,17},{3,18},{4,19},{5,20},{6,21},{7,22},{8,23},{9,... | collective-permute-start | bytes 147464 | tf_op jit(solution)/shard_map/ppermute | solution.py:44
  55.6 4.2 %collective-permute-start.9 = (f32[32,192]{1,0:T(8,128)S(1)}, f32[32,192]{1,0:T(8,128)S(1)}, u32[]{:S(2)}, u32[]{:S(2)}) collective-permute-start(f32[32,192]{1,0:T(8,128)S(1)} %get-tuple-element.29.refs_3_.ho), channel_id=1, source_target_pairs={{0,16},{1,17},{2,18},{3,19},{4,20},{5,21},{6,22},{7,23},{8,24},{9,... | collective-permute-start | bytes 73736 | tf_op jit(solution)/shard_map/ppermute | solution.py:44
